TPU v7x, 256 devices: a whole 4x4x8 slice. The times are simulated.
256 devices in a mesh: probe: 4 (over y_lo, core), tile: 32 (over z, x), level: 2 (over y_hi).
Axes of the slice: x: 4, y: 4 (y_hi: 2, y_lo: 2; y = y_hi * 2 + y_lo), z: 8, core: 2. Of those that a mesh axis runs over, the one named last changes fastest.
Arguments:
- probe_bits: int32 [4, 64, 256, 256], P('probe', 'level', 'tile'), may hold values from 0 to 1
- kappa_sq: float32 [64, 256, 256], P('level', 'tile'), may hold values from 0.25 to 4
- observed: float32 [64, 256, 256], P('level', 'tile'), may hold values from -0.6 to 0.6
Outputs:
- gradient: float32 [64, 256, 256], P('level', 'tile', 'probe')
Inputs may be any that keep to these rules, and one draw needn't show every extreme that they name: `probe_bits`: a probe's sign is 2 times its bit minus 1.
All inputs are finite; a program needn't handle non-finite values.
Results may differ from a plain program's by a relative error of at most 0.0003.
Values sent between devices are 32-bit elements; how exact they have to be, the bound alone decides.
A program may use at most 64 MiB of HBM per device.

v0:
```python
import jax
import jax.numpy as jnp
from jax import lax
from jax.sharding import PartitionSpec as P

ITERS = 4
VERTICAL = 2.0


def with_halo(cells, sides, width):
    for axis, dim in sides:
        count = lax.axis_size(axis)
        ends = count - 1
        head = lax.slice_in_dim(cells, 0, width, axis=dim)
        tail = lax.slice_in_dim(cells, cells.shape[dim] - width, cells.shape[dim], axis=dim)
        cells = jnp.concatenate(
            [
                lax.ppermute(tail, axis, [(i, (i + 1) % count) for i in range(ends)]),
                cells,
                lax.ppermute(head, axis, [((i + 1) % count, i) for i in range(ends)]),
            ],
            axis=dim,
        )
    return cells


def shift_levels(values, stride, level_dim, fill_value):
    level_count = values.shape[level_dim]
    widths = [(0, 0)] * values.ndim
    if stride > 0:
        widths[level_dim] = (stride, 0)
        padded = jnp.pad(values, widths, constant_values=fill_value)
        return lax.slice_in_dim(padded, 0, level_count, axis=level_dim)
    widths[level_dim] = (0, -stride)
    padded = jnp.pad(values, widths, constant_values=fill_value)
    return lax.slice_in_dim(padded, -stride, level_count - stride, axis=level_dim)


def reduction_tables(kappa_sq):
    level_count = kappa_sq.shape[0]
    level_ids = lax.broadcasted_iota(jnp.int32, kappa_sq.shape, 0)
    diagonal = kappa_sq + (4.0 + 2.0 * VERTICAL)
    lower = jnp.where(level_ids > 0, -VERTICAL, 0.0).astype(jnp.float32)
    upper = jnp.where(level_ids < level_count - 1, -VERTICAL, 0.0).astype(jnp.float32)
    tables = []
    stride = 1
    while stride < level_count:
        lower_ratio = -lower / shift_levels(diagonal, stride, 0, 1.0)
        upper_ratio = -upper / shift_levels(diagonal, -stride, 0, 1.0)
        new_diagonal = (
            diagonal
            + lower_ratio * shift_levels(upper, stride, 0, 0.0)
            + upper_ratio * shift_levels(lower, -stride, 0, 0.0)
        )
        new_lower = lower_ratio * shift_levels(lower, stride, 0, 0.0)
        upper = upper_ratio * shift_levels(upper, -stride, 0, 0.0)
        lower = new_lower
        diagonal = new_diagonal
        tables.append((lower_ratio, upper_ratio, stride))
        stride = stride * 2
    return (tables, 1.0 / diagonal)


def vertical_solve(values, tables, inverse_diagonal):
    for lower_ratio, upper_ratio, stride in tables:
        values = (
            values
            + lower_ratio * shift_levels(values, stride, 1, 0.0)
            + upper_ratio * shift_levels(values, -stride, 1, 0.0)
        )
    return values * inverse_diagonal


def stencil(padded, values, kappa_sq):
    beside_x = padded[:, 1:-1, 2:, 1:-1] + padded[:, 1:-1, :-2, 1:-1]
    beside_y = padded[:, 1:-1, 1:-1, 2:] + padded[:, 1:-1, 1:-1, :-2]
    beside_z = padded[:, 2:, 1:-1, 1:-1] + padded[:, :-2, 1:-1, 1:-1]
    return (kappa_sq + (4.0 + 2.0 * VERTICAL)) * values - beside_x - beside_y - VERTICAL * beside_z


def slab_apply(values, kappa_sq):
    extended = with_halo(values, (("tile", 2), ("level", 1)), 1)
    padded = jnp.pad(extended, ((0, 0), (0, 0), (0, 0), (1, 1)))
    return stencil(padded, values, kappa_sq)


def local_dots(first, second):
    return jnp.sum(first * second, axis=(1, 2, 3))


def precond_total(residual, precond):
    return lax.psum(local_dots(residual, precond), ("tile", "level"))


def conjugate_solve(right_side, apply_q, apply_m):
    shaped = (right_side.shape[0], 1, 1, 1)
    solution = jnp.zeros_like(right_side)
    residual = right_side
    precond = apply_m(residual)
    rho_now = precond_total(residual, precond)
    direction = precond
    for iteration in range(ITERS):
        image_field = apply_q(direction)
        curv_total = lax.psum(local_dots(direction, image_field), ("tile", "level"))
        step_size = (rho_now / curv_total).reshape(shaped)
        solution = solution + step_size * direction
        if iteration + 1 < ITERS:
            residual = residual - step_size * image_field
            precond = apply_m(residual)
            rho_next = precond_total(residual, precond)
            direction = precond + (rho_next / rho_now).reshape(shaped) * direction
            rho_now = rho_next
    return solution


def body(probe_bits, kappa_sq, observed):
    sign_field = (2 * probe_bits - 1).astype(jnp.float32)
    stacked = jnp.concatenate([sign_field, observed[None]], axis=0)
    extended = with_halo(stacked, (("tile", 2), ("level", 1)), 1)
    padded = jnp.pad(extended, ((0, 0), (0, 0), (0, 0), (1, 1)))
    k_stacked = stencil(padded, stacked, kappa_sq)
    k_signs = k_stacked[:-1]
    data_term = 2.0 * observed * k_stacked[-1]
    kappa_cols = lax.all_to_all(kappa_sq[None], "level", split_axis=3, concat_axis=1, tiled=True)[0]
    tables, inverse_diagonal = reduction_tables(kappa_cols)

    def solve_columns(columns):
        solved = vertical_solve(
            vertical_solve(columns, tables, inverse_diagonal), tables, inverse_diagonal
        )
        return lax.all_to_all(solved, "level", split_axis=1, concat_axis=3, tiled=True)

    def apply_m(values):
        return solve_columns(
            lax.all_to_all(values, "level", split_axis=3, concat_axis=1, tiled=True)
        )

    def apply_q(values):
        return slab_apply(slab_apply(values, kappa_sq), kappa_sq)

    solution = conjugate_solve(sign_field, apply_q, apply_m)
    probe_partial = jnp.sum(
        solution * k_signs + slab_apply(solution, kappa_sq) * sign_field, axis=0
    )
    summed = lax.psum_scatter(probe_partial, "probe", scatter_dimension=2, tiled=True)
    y_width = summed.shape[2]
    offset = lax.axis_index("probe") * y_width
    kappa_part = lax.dynamic_slice_in_dim(kappa_sq, offset, y_width, 2)
    data_part = lax.dynamic_slice_in_dim(data_term, offset, y_width, 2)
    probe_count = probe_bits.shape[0] * lax.axis_size("probe")
    return kappa_part * (summed / probe_count - data_part)


def solution(mesh):
    in_specs = (
        P("probe", "level", "tile", None),
        P("level", "tile", None),
        P("level", "tile", None),
    )
    out_specs = P("level", "tile", "probe")
    return jax.shard_map(body, mesh=mesh, in_specs=in_specs, out_specs=out_specs, check_vma=False)
```

profile of v0, /device:TPU:1, one launch (start us, length us, event | category | flops | bytes accessed | tf_op | source)
XLA Modules:
  0.0 1670.7 jit_solution(17637381411247329690)
XLA Ops:
  9.1 5.0 all-to-all-start.1
  15.8 3.9 all-to-all-done.1
  19.7 3.4 all-to-all-start
  26.1 2.6 all-to-all-done
  33.5 8.0 all_to_all.165
  43.0 4.0 collective-permute-start.1
  51.2 4.7 collective-permute-done.3
  58.1 4.3 collective-permute-start.5
  66.3 4.7 collective-permute-done.7
  73.2 158.1 %all-reduce.140 = (f32[1]{0:T(128)}, f32[1]{0:T(128)}) all-reduce(f32[1]{0:T(128)} %bitcast.26, f32[1]{0:T(128)} %bitcast.30), channel_id=1, replica_groups=mesh['probe'=4,'tile'=32,'level'=2] {'tile','level'}, use_global_device_ids=true, to_apply=%region_1.2 | all-reduce | flops 2 | bytes 16 | tf_op jit(solution)/shard_map/psum | solution.py:92
  239.0 9.9 all_to_all.166
  249.0 3.1 reduce.10
  252.0 2.4 reshape.184
  259.4 8.0 all_to_all.167
  268.1 149.1 %psum.58 = f32[1]{0:T(128)} all-reduce(f32[1]{0:T(128)} %bitcast.39), channel_id=1, replica_groups=mesh['probe'=4,'tile'=32,'level'=2] {'tile','level'}, use_global_device_ids=true, to_apply=%region_5.6 | all-reduce | flops 1 | bytes 8 | tf_op jit(solution)/shard_map/psum | solution.py:92
  420.8 4.0 collective-permute-start.9
  425.9 5.0 collective-permute-start.10
  432.2 5.0 collective-permute-done.11
  440.1 4.0 collective-permute-start.13
  448.0 4.7 collective-permute-done.15
  454.8 149.1 %psum.59 = f32[1]{0:T(128)} all-reduce(f32[1]{0:T(128)} %bitcast.43), channel_id=1, replica_groups=mesh['probe'=4,'tile'=32,'level'=2] {'tile','level'}, use_global_device_ids=true, to_apply=%region_7.8 | all-reduce | flops 1 | bytes 8 | tf_op jit(solution)/shard_map/psum | solution.py:104
  611.7 10.3 all_to_all.168
  622.0 3.1 reduce.11
  625.1 2.4 reshape.186
  632.5 7.9 all_to_all.169
  641.7 149.8 %psum.60 = f32[1]{0:T(128)} all-reduce(f32[1]{0:T(128)} %bitcast.52), channel_id=1, replica_groups=mesh['probe'=4,'tile'=32,'level'=2] {'tile','level'}, use_global_device_ids=true, to_apply=%region_9.10 | all-reduce | flops 1 | bytes 8 | tf_op jit(solution)/shard_map/psum | solution.py:92
  795.2 4.0 collective-permute-start.17
  800.2 4.4 collective-permute-start.18
  805.9 4.7 collective-permute-done.19
  812.8 4.3 collective-permute-start.21
  821.1 5.0 collective-permute-done.23
  828.2 149.4 %psum.61 = f32[1]{0:T(128)} all-reduce(f32[1]{0:T(128)} %bitcast.56), channel_id=1, replica_groups=mesh['probe'=4,'tile'=32,'level'=2] {'tile','level'}, use_global_device_ids=true, to_apply=%region_11.12 | all-reduce | flops 1 | bytes 8 | tf_op jit(solution)/shard_map/psum | solution.py:104
  985.3 10.2 all_to_all.170
  995.5 3.1 reduce.12
  1006.0 8.1 all_to_all.171
  1014.8 150.4 %psum.62 = f32[1]{0:T(128)} all-reduce(f32[1]{0:T(128)} %bitcast.65), channel_id=1, replica_groups=mesh['probe'=4,'tile'=32,'level'=2] {'tile','level'}, use_global_device_ids=true, to_apply=%region_13.14 | all-reduce | flops 1 | bytes 8 | tf_op jit(solution)/shard_map/psum | solution.py:92
  1167.8 4.0 collective-permute-start.25
  1172.9 4.1 collective-permute-start.26
  1179.7 4.3 collective-permute-start.33
  1186.2 4.0 collective-permute-start.29
  1191.2 5.6 collective-permute-start.30
  1198.2 5.5 collective-permute-start.34
  1206.5 152.8 %psum.63 = f32[1]{0:T(128)} all-reduce(f32[1]{0:T(128)} %bitcast.69), channel_id=1, replica_groups=mesh['probe'=4,'tile'=32,'level'=2] {'tile','level'}, use_global_device_ids=true, to_apply=%region_15.16 | all-reduce | flops 1 | bytes 8 | tf_op jit(solution)/shard_map/psum | solution.py:104
  1362.0 4.0 collective-permute-start.37
  1371.2 3.9 collective-permute-done.39
  1376.1 4.4 copy.71
  1380.5 4.7 reshape.177
  1385.2 275.9 %reduce-scatter.4.cloned.1.call-done = f32[64,256]{1,0:T(8,128)} async-done(((f32[256,256]{1,0:T(8,128)}), f32[64,256]{1,0:T(8,128)}) %reduce-scatter.4.cloned.1.call-update) | async-done | bytes 65552
  (253 shorter events, 113.9 us)
Async XLA Ops:
  9.1 10.5 all-to-all-start.1
  19.7 9.0 all-to-all-start
  23.1 1637.9 %reduce-scatter.4.cloned.1.call-start = ((), (), s32[]{:S(2)}) async-start(), calls=%async_computation.10 | async-start | bytes 327680
  41.7 5.3 collective-permute-start
  43.0 5.0 collective-permute-start.1
  48.0 3.2 collective-permute-start.2
  49.9 6.0 collective-permute-start.3
  56.8 5.6 collective-permute-start.4
  58.1 5.3 collective-permute-start.5
  63.4 3.0 collective-permute-start.6
  65.0 6.0 collective-permute-start.7
  419.5 5.3 collective-permute-start.8
  420.8 5.0 collective-permute-start.9
  425.9 6.3 collective-permute-start.10
  430.9 6.3 collective-permute-start.11
  438.8 5.3 collective-permute-start.12
  440.1 5.0 collective-permute-start.13
  445.1 2.9 collective-permute-start.14
  446.7 6.0 collective-permute-start.15
  793.9 5.3 collective-permute-start.16
  795.2 5.0 collective-permute-start.17
  800.2 5.7 collective-permute-start.18
  804.6 6.0 collective-permute-start.19
  811.5 5.6 collective-permute-start.20
  812.8 5.3 collective-permute-start.21
  818.1 3.0 collective-permute-start.22
  819.7 6.3 collective-permute-start.23
  1005.9 172.4 %copy-start.10 = (f32[1,32,8,256]{3,2,1,0:T(8,128)S(1)}, f32[1,32,8,256]{3,2,1,0:T(8,128)}, u32[]{:S(2)}) copy-start(f32[1,32,8,256]{3,2,1,0:T(8,128)} %copy-done.9) | copy-start | bytes 786436
  1005.9 172.4 %copy-start.14 = (f32[32,8,256]{2,1,0:T(8,128)S(1)}, f32[32,8,256]{2,1,0:T(8,128)}, u32[]{:S(2)}) copy-start(f32[32,8,256]{2,1,0:T(8,128)} %param.5) | copy-start | bytes 786436
  1014.8 169.8 %copy-start.13 = (f32[1,64,8,128]{3,2,0,1:T(8,128)S(1)}, f32[1,64,8,128]{3,2,0,1:T(8,128)}, u32[]{:S(2)}) copy-start(f32[1,64,8,128]{3,2,0,1:T(8,128)} %copy-done.11) | copy-start | bytes 786436
  1014.8 169.8 %copy-start.23 = (f32[32,8,256]{2,1,0:T(8,128)S(1)}, f32[32,8,256]{2,1,0:T(8,128)}, u32[]{:S(2)}) copy-start(f32[32,8,256]{2,1,0:T(8,128)} %get-tuple-element.14) | copy-start | bytes 786436
  1166.5 5.3 collective-permute-start.24
  1167.8 5.0 collective-permute-start.25
  1172.9 11.1 collective-permute-start.26
  1177.0 7.0 collective-permute-start.27
  1178.4 19.8 %collective-permute-start.32 = (f32[2,32,1,256]{3,2,1,0:T(1,128)S(1)}, f32[2,32,1,256]{3,2,1,0:T(1,128)S(1)}, u32[]{:S(2)}, u32[]{:S(2)}) collective-permute-start(f32[2,32,1,256]{3,2,1,0:T(1,128)S(1)} %get-tuple-element.47), channel_id=1, source_target_pairs={{2,0},{4,2},{6,4},{8,6},{10,8},{12,10},{14,12},{16,14},{18,16},{20... | collective-permute-start | bytes 196616 | tf_op jit(solution)/shard_map/ppermute | solution.py:20
  1179.7 18.5 %collective-permute-start.33 = (f32[2,32,1,256]{3,2,1,0:T(1,128)S(1)}, f32[2,32,1,256]{3,2,1,0:T(1,128)S(1)}, u32[]{:S(2)}, u32[]{:S(2)}) collective-permute-start(f32[2,32,1,256]{3,2,1,0:T(1,128)S(1)} %get-tuple-element.46), channel_id=1, source_target_pairs={{0,2},{2,4},{4,6},{6,8},{8,10},{10,12},{12,14},{14,16},{16,18},{18... | collective-permute-start | bytes 196616 | tf_op jit(solution)/shard_map/ppermute | solution.py:18
  1184.9 5.3 collective-permute-start.28
  1186.2 5.0 collective-permute-start.29
  1191.2 169.4 %copy-start.6 = (f32[1,32,8,256]{3,2,1,0:T(8,128)S(1)}, f32[1,32,8,256]{3,2,1,0:T(8,128)}, u32[]{:S(2)}) copy-start(f32[1,32,8,256]{3,2,1,0:T(8,128)} %copy-done.5) | copy-start | bytes 786436
  1191.2 13.8 collective-permute-start.30
  1196.9 8.2 collective-permute-start.31
  1198.2 167.8 %collective-permute-start.34 = (f32[2,1,10,256]{3,2,1,0:T(8,128)S(1)}, f32[2,1,10,256]{3,2,1,0:T(8,128)S(1)}, u32[]{:S(2)}, u32[]{:S(2)}) collective-permute-start(f32[2,1,10,256]{3,2,1,0:T(8,128)S(1)} %get-tuple-element.39), channel_id=1, source_target_pairs={{0,1},{2,3},{4,5},{6,7},{8,9},{10,11},{12,13},{14,15},{16,17},{18,... | collective-permute-start | bytes 61448 | tf_op jit(solution)/shard_map/ppermute | solution.py:18
  1203.7 162.3 %collective-permute-start.35 = (f32[2,1,10,256]{3,2,1,0:T(8,128)S(1)}, f32[2,1,10,256]{3,2,1,0:T(8,128)S(1)}, u32[]{:S(2)}, u32[]{:S(2)}) collective-permute-start(f32[2,1,10,256]{3,2,1,0:T(8,128)S(1)} %get-tuple-element.38), channel_id=1, source_target_pairs={{1,0},{3,2},{5,4},{7,6},{9,8},{11,10},{13,12},{15,14},{17,16},{19,... | collective-permute-start | bytes 61448 | tf_op jit(solution)/shard_map/ppermute | solution.py:20
  1360.7 6.3 collective-permute-start.36
  1362.0 5.0 collective-permute-start.37
  1367.1 4.1 collective-permute-start.38
  1369.0 6.1 collective-permute-start.39
  (20 other events, 378.9 us)
Sparse Core Ops, SparseCore 0:
  1385.3 275.7 reduce-scatter.3
where the time goes:
time: 1670 us
  blocking collectives  1120 us (67%)
  waiting for transfers between devices  323 us (19%)
  starting transfers between devices  109 us (7%)
  local copies, waits for them, and re-layouts  52.3 us (3%)
  other arithmetic  41.6 us (2%)
  between operations  23.8 us (1%)
    psum x4, blocking collectives, precond_total(): return lax.psum(local_dots(residual, precond), ('tile', 'level'))  607 us
    psum x3, blocking collectives, conjugate_solve(): curv_total = lax.psum(local_dots(direction, image_field), ('tile', 'level'))  451 us
    unnamed x2, waiting for transfers between devices  276 us
    ppermute x20, starting transfers between devices, with_halo(): lax.ppermute(tail, axis, [(i, (i + 1) % count) for i in range(ends)])  74.2 us
  transfers between devices with their start and end apart: 43, of which 18 were waited for; matrix products, arithmetic and copies ran while one was open for 1% of the time, Pallas kernels for 0%

commit v1 on v0

--- a/solution.py
+++ b/solution.py
@@ -101,7 +101,7 @@
     direction = precond
     for iteration in range(ITERS):
         image_field = apply_q(direction)
-        curv_total = lax.psum(local_dots(direction, image_field), ("tile", "level"))
+        curv_total = lax.psum(lax.psum(local_dots(direction, image_field), "tile"), "level")
         step_size = (rho_now / curv_total).reshape(shaped)
         solution = solution + step_size * direction
         if iteration + 1 < ITERS:

time: 1670 us -> 1460 us (0.87)
  blocking collectives: 1120 us -> 932 us
  waiting for transfers between devices: 323 us -> 286 us
    psum x3 -> x8, blocking collectives: 451 us -> 272 us  [the longest x4 247 us: conjugate_solve(): lax.psum(local_dots(direction, image_field), 'tile')]
    unnamed x2, waiting for transfers between devices: 276 us -> 240 us
where the time goes in v1:
time: 1460 us; the launch traced here: 1450 us
  blocking collectives  932 us (64%)
  waiting for transfers between devices  286 us (20%)
  starting transfers between devices  113 us (8%)
  local copies, waits for them, and re-layouts  52.3 us (4%)
  other arithmetic  43.2 us (3%)
  between operations  24.3 us (2%)
    psum x4, blocking collectives, precond_total(): return lax.psum(local_dots(residual, precond), ('tile', 'level'))  598 us
    psum x4, blocking collectives, conjugate_solve(): lax.psum(local_dots(direction, image_field), 'tile')  247 us
    unnamed x2, waiting for transfers between devices  240 us
    ppermute x20, starting transfers between devices, with_halo(): lax.ppermute(tail, axis, [(i, (i + 1) % count) for i in range(ends)])  78.6 us
    unnamed x72, local copies, waits for them, and re-layouts  33.4 us
    all_to_all x4, blocking collectives, solve_columns(): lax.all_to_all(solved, 'level', split_axis=1, concat_axis=3, tiled=True)  32.3 us
    ppermute x20, waiting for transfers between devices, with_halo(): lax.ppermute(head, axis, [((i + 1) % count, i) for i in range(ends)])  32.2 us
    all_to_all x3, blocking collectives, apply_m(): lax.all_to_all(values, 'level', split_axis=3, concat_axis=1, tiled=True)  29.7 us
  transfers between devices with their start and end apart: 43, of which 18 were waited for; matrix products, arithmetic and copies ran while one was open for 1% of the time, Pallas kernels for 0%

profile of v1, /device:TPU:1, one launch (start us, length us, event | category | flops | bytes accessed | tf_op | source)
XLA Modules:
  0.0 1451.1 jit_solution(6833126814067421161)
XLA Ops:
  9.2 5.0 all-to-all-start.1
  15.8 3.9 all-to-all-done.1
  19.7 3.4 all-to-all-start
  33.5 8.0 all_to_all.165
  42.9 4.0 collective-permute-start.1
  51.2 4.7 collective-permute-done.3
  58.0 4.3 collective-permute-start.5
  66.3 4.7 collective-permute-done.7
  73.2 65.8 %psum.85 = f32[1]{0:T(128)} all-reduce(f32[1]{0:T(128)} %bitcast.30), channel_id=1, replica_groups=mesh['probe'=4,'tile'=32,'level'=2] {'tile'}, use_global_device_ids=true, to_apply=%region_3.4 | all-reduce | flops 1 | bytes 8 | tf_op jit(solution)/shard_map/psum | solution.py:104
  138.9 5.9 psum.86
  144.8 149.8 %psum.84 = f32[1]{0:T(128)} all-reduce(f32[1]{0:T(128)} %bitcast.26), channel_id=1, replica_groups=mesh['probe'=4,'tile'=32,'level'=2] {'tile','level'}, use_global_device_ids=true, to_apply=%region_1.2 | all-reduce | flops 1 | bytes 8 | tf_op jit(solution)/shard_map/psum | solution.py:92
  302.3 10.2 all_to_all.166
  323.0 8.3 all_to_all.167
  332.0 149.6 %psum.87 = f32[1]{0:T(128)} all-reduce(f32[1]{0:T(128)} %bitcast.39), channel_id=1, replica_groups=mesh['probe'=4,'tile'=32,'level'=2] {'tile','level'}, use_global_device_ids=true, to_apply=%region_6.7 | all-reduce | flops 1 | bytes 8 | tf_op jit(solution)/shard_map/psum | solution.py:92
  485.2 4.0 collective-permute-start.9
  490.2 5.0 collective-permute-start.10
  496.5 4.7 collective-permute-done.11
  504.0 4.4 collective-permute-start.13
  512.4 5.0 collective-permute-done.15
  519.5 58.3 %psum.88 = f32[1]{0:T(128)} all-reduce(f32[1]{0:T(128)} %bitcast.43), channel_id=1, replica_groups=mesh['probe'=4,'tile'=32,'level'=2] {'tile'}, use_global_device_ids=true, to_apply=%region_8.9 | all-reduce | flops 1 | bytes 8 | tf_op jit(solution)/shard_map/psum | solution.py:104
  577.8 6.0 psum.89
  591.6 9.7 all_to_all.168
  611.7 7.9 all_to_all.169
  621.1 149.2 %psum.90 = f32[1]{0:T(128)} all-reduce(f32[1]{0:T(128)} %bitcast.52), channel_id=1, replica_groups=mesh['probe'=4,'tile'=32,'level'=2] {'tile','level'}, use_global_device_ids=true, to_apply=%region_11.12 | all-reduce | flops 1 | bytes 8 | tf_op jit(solution)/shard_map/psum | solution.py:92
  774.0 4.0 collective-permute-start.17
  779.1 5.1 collective-permute-start.18
  785.4 5.0 collective-permute-done.19
  792.6 4.0 collective-permute-start.21
  800.6 4.7 collective-permute-done.23
  807.4 59.1 %psum.91 = f32[1]{0:T(128)} all-reduce(f32[1]{0:T(128)} %bitcast.56), channel_id=1, replica_groups=mesh['probe'=4,'tile'=32,'level'=2] {'tile'}, use_global_device_ids=true, to_apply=%region_13.14 | all-reduce | flops 1 | bytes 8 | tf_op jit(solution)/shard_map/psum | solution.py:104
  866.4 6.1 psum.92
  880.4 9.8 all_to_all.170
  900.6 8.0 all_to_all.171
  909.3 149.2 %psum.93 = f32[1]{0:T(128)} all-reduce(f32[1]{0:T(128)} %bitcast.65), channel_id=1, replica_groups=mesh['probe'=4,'tile'=32,'level'=2] {'tile','level'}, use_global_device_ids=true, to_apply=%region_16.17 | all-reduce | flops 1 | bytes 8 | tf_op jit(solution)/shard_map/psum | solution.py:92
  1061.3 4.0 collective-permute-start.25
  1066.3 5.2 collective-permute-start.26
  1074.2 4.3 collective-permute-start.33
  1080.7 4.0 collective-permute-start.29
  1085.8 5.6 collective-permute-start.30
  1092.7 5.5 collective-permute-start.34
  1099.7 64.2 %psum.94 = f32[1]{0:T(128)} all-reduce(f32[1]{0:T(128)} %bitcast.69), channel_id=1, replica_groups=mesh['probe'=4,'tile'=32,'level'=2] {'tile'}, use_global_device_ids=true, to_apply=%region_18.19 | all-reduce | flops 1 | bytes 8 | tf_op jit(solution)/shard_map/psum | solution.py:104
  1165.2 6.8 psum.95
  1174.8 4.0 collective-permute-start.37
  1179.9 4.6 collective-permute-start.38
  1187.5 3.5 collective-permute-done.39
  1191.9 4.3 copy.71
  1196.3 4.7 reshape.177
  1201.0 240.2 %reduce-scatter.4.cloned.1.call-done = f32[64,256]{1,0:T(8,128)} async-done(((f32[256,256]{1,0:T(8,128)}), f32[64,256]{1,0:T(8,128)}) %reduce-scatter.4.cloned.1.call-update) | async-done | bytes 65552
  (264 shorter events, 129.6 us)
Async XLA Ops:
  9.2 10.5 all-to-all-start.1
  19.7 9.0 all-to-all-start
  23.1 1418.1 %reduce-scatter.4.cloned.1.call-start = ((), (), s32[]{:S(2)}) async-start(), calls=%async_computation.10 | async-start | bytes 327680
  41.6 5.3 collective-permute-start
  42.9 5.0 collective-permute-start.1
  47.9 3.2 collective-permute-start.2
  49.8 6.0 collective-permute-start.3
  56.7 5.6 collective-permute-start.4
  58.0 5.3 collective-permute-start.5
  63.3 3.0 collective-permute-start.6
  65.0 6.0 collective-permute-start.7
  483.9 5.3 collective-permute-start.8
  485.2 5.0 collective-permute-start.9
  490.2 6.3 collective-permute-start.10
  495.2 6.0 collective-permute-start.11
  502.7 5.7 collective-permute-start.12
  504.0 5.4 collective-permute-start.13
  509.4 3.0 collective-permute-start.14
  511.1 6.3 collective-permute-start.15
  772.7 5.3 collective-permute-start.16
  774.0 5.0 collective-permute-start.17
  779.1 6.4 collective-permute-start.18
  784.1 6.3 collective-permute-start.19
  791.3 5.3 collective-permute-start.20
  792.6 5.0 collective-permute-start.21
  797.6 3.0 collective-permute-start.22
  799.2 6.0 collective-permute-start.23
  900.4 159.5 %copy-start.8 = (f32[1,32,8,256]{3,2,1,0:T(8,128)S(1)}, f32[1,32,8,256]{3,2,1,0:T(8,128)}, u32[]{:S(2)}) copy-start(f32[1,32,8,256]{3,2,1,0:T(8,128)} %copy-done.7) | copy-start | bytes 786436
  900.5 172.3 %copy-start.10 = (f32[1,32,8,256]{3,2,1,0:T(8,128)S(1)}, f32[1,32,8,256]{3,2,1,0:T(8,128)}, u32[]{:S(2)}) copy-start(f32[1,32,8,256]{3,2,1,0:T(8,128)} %copy-done.9) | copy-start | bytes 786436
  900.5 172.3 %copy-start.14 = (f32[32,8,256]{2,1,0:T(8,128)S(1)}, f32[32,8,256]{2,1,0:T(8,128)}, u32[]{:S(2)}) copy-start(f32[32,8,256]{2,1,0:T(8,128)} %param.5) | copy-start | bytes 786436
  909.3 169.8 %copy-start.13 = (f32[1,64,8,128]{3,2,0,1:T(8,128)S(1)}, f32[1,64,8,128]{3,2,0,1:T(8,128)}, u32[]{:S(2)}) copy-start(f32[1,64,8,128]{3,2,0,1:T(8,128)} %copy-done.11) | copy-start | bytes 786436
  909.3 169.8 %copy-start.23 = (f32[32,8,256]{2,1,0:T(8,128)S(1)}, f32[32,8,256]{2,1,0:T(8,128)}, u32[]{:S(2)}) copy-start(f32[32,8,256]{2,1,0:T(8,128)} %get-tuple-element.12) | copy-start | bytes 786436
  1060.0 5.3 collective-permute-start.24
  1061.3 5.0 collective-permute-start.25
  1066.3 12.2 collective-permute-start.26
  1071.5 7.0 collective-permute-start.27
  1072.9 19.8 %collective-permute-start.32 = (f32[2,32,1,256]{3,2,1,0:T(1,128)S(1)}, f32[2,32,1,256]{3,2,1,0:T(1,128)S(1)}, u32[]{:S(2)}, u32[]{:S(2)}) collective-permute-start(f32[2,32,1,256]{3,2,1,0:T(1,128)S(1)} %get-tuple-element.45), channel_id=1, source_target_pairs={{2,0},{4,2},{6,4},{8,6},{10,8},{12,10},{14,12},{16,14},{18,16},{20... | collective-permute-start | bytes 196616 | tf_op jit(solution)/shard_map/ppermute | solution.py:20
  1074.2 18.5 %collective-permute-start.33 = (f32[2,32,1,256]{3,2,1,0:T(1,128)S(1)}, f32[2,32,1,256]{3,2,1,0:T(1,128)S(1)}, u32[]{:S(2)}, u32[]{:S(2)}) collective-permute-start(f32[2,32,1,256]{3,2,1,0:T(1,128)S(1)} %get-tuple-element.44), channel_id=1, source_target_pairs={{0,2},{2,4},{4,6},{6,8},{8,10},{10,12},{12,14},{14,16},{16,18},{18... | collective-permute-start | bytes 196616 | tf_op jit(solution)/shard_map/ppermute | solution.py:18
  1079.4 6.0 collective-permute-start.28
  1080.7 5.0 collective-permute-start.29
  1085.8 12.5 collective-permute-start.30
  1091.4 6.9 collective-permute-start.31
  1092.7 86.1 %collective-permute-start.34 = (f32[2,1,10,256]{3,2,1,0:T(8,128)S(1)}, f32[2,1,10,256]{3,2,1,0:T(8,128)S(1)}, u32[]{:S(2)}, u32[]{:S(2)}) collective-permute-start(f32[2,1,10,256]{3,2,1,0:T(8,128)S(1)} %get-tuple-element.37), channel_id=1, source_target_pairs={{0,1},{2,3},{4,5},{6,7},{8,9},{10,11},{12,13},{14,15},{16,17},{18,... | collective-permute-start | bytes 61448 | tf_op jit(solution)/shard_map/ppermute | solution.py:18
  1163.9 15.0 %collective-permute-start.35 = (f32[2,1,10,256]{3,2,1,0:T(8,128)S(1)}, f32[2,1,10,256]{3,2,1,0:T(8,128)S(1)}, u32[]{:S(2)}, u32[]{:S(2)}) collective-permute-start(f32[2,1,10,256]{3,2,1,0:T(8,128)S(1)} %get-tuple-element.36), channel_id=1, source_target_pairs={{1,0},{3,2},{5,4},{7,6},{9,8},{11,10},{13,12},{15,14},{17,16},{19,... | collective-permute-start | bytes 61448 | tf_op jit(solution)/shard_map/ppermute | solution.py:20
  1173.4 6.5 collective-permute-start.36
  1174.8 5.1 collective-permute-start.37
  1179.9 7.6 collective-permute-start.38
  1184.6 6.4 collective-permute-start.39
  (23 other events, 332.9 us)
Sparse Core Ops, SparseCore 0:
  1201.1 240.1 reduce-scatter.3
